TPU v7x, 32 devices: a whole 2x2x4 slice. The times are simulated.
32 devices in a mesh: gx: 8 (over y, x, core), gy: 4 (over z).
Axes of the slice: x: 2, y: 2, z: 4, core: 2. Of those that a mesh axis runs over, the one named last changes fastest.
Arguments:
- distribution: float32 [8, 32, 32768], P('gx', 'gy'), may hold values from 0.2 to 2
- relax_rate: float32 [8, 32], P('gx', 'gy'), may hold values from 0.05 to 0.8
- block_level: int32 [8], replicated, may hold values from 0 to 1, as said below
- block_link: int32 [2, 64], replicated, may hold values from 0 to 7, as said below
- remap_values: bfloat16 [2, 64, 512, 512], P(None, 'gy'), may hold values from -0.25 to 0.25
Outputs:
- updated: float32 [8, 32, 32768], P('gx', 'gy')
Inputs may be any that keep to these rules, and one draw needn't show every extreme that they name: `block_level`: every maximal run of streamwise blocks with one level holds at least two blocks; the first run holds exactly two, so the level changes between blocks 1 and 2. `block_link`: in each direction every coarse block is named by exactly 8 fine blocks.
All inputs are finite; a program needn't handle non-finite values.
Results may differ from a plain program's by a relative error of at most 0.00095.
Values may be sent and summed in bfloat16 or wider, within the bound.
No kernel may reach another device: no remote copies, remote signals or barrier semaphores. Data moves between devices by JAX's collectives and lax.ppermute only.
A program may use at most 64 MiB of HBM per device.

v0:
```python
import math

import jax
import jax.numpy as jnp
from jax import lax
from jax.sharding import PartitionSpec as P

SC = 16
SF = 32
BLK = 512
NVC = 4096
NVF = 32768
VBF = 64


cfl_ratio = 0.03
spacing_coarse = 0.5
spacing_fine = 0.4


def with_halo(value, sides, width):
    for axis, dim in sides:
        size, length = (lax.axis_size(axis), value.shape[dim])
        up = [(i, (i + 1) % size) for i in range(size - 1)]
        down = [(j, i) for i, j in up]
        last = lax.slice_in_dim(value, length - width, length, axis=dim)
        leading = lax.slice_in_dim(value, 0, width, axis=dim)
        before = lax.ppermute(last, axis, up)
        after = lax.ppermute(leading, axis, down)
        value = jnp.concatenate([before, value, after], axis=dim)
    return value


def velocity_tables(level, points):
    position = jnp.arange(points, dtype=jnp.int32)
    side = jnp.where(level == 1, SF, SC).astype(jnp.int32)
    spacing = jnp.where(level == 1, spacing_fine, spacing_coarse).astype(jnp.float32)
    centre = (side - 1).astype(jnp.float32) * 0.5
    along_x = spacing * ((position // (side * side)).astype(jnp.float32) - centre)
    along_y = spacing * ((position // side % side).astype(jnp.float32) - centre)
    along_z = spacing * ((position % side).astype(jnp.float32) - centre)
    valid = position < side * side * side
    return (along_x, along_y, along_z, valid, spacing)


def relax_update(distribution, relax_rate, level, from_lower, from_upper, from_left, from_right):
    points = distribution.shape[-1]
    along_x, along_y, along_z, valid, spacing = velocity_tables(level, points)
    weight = spacing * spacing * spacing
    masked = jnp.where(valid, distribution, 0.0)
    particle_count_field = weight * jnp.sum(masked, -1)
    mean_flow_first_axis = weight * jnp.sum(masked * along_x, -1) / particle_count_field
    mean_flow_second_axis = weight * jnp.sum(masked * along_y, -1) / particle_count_field
    mean_flow_third_axis = weight * jnp.sum(masked * along_z, -1) / particle_count_field
    motion_squared_half = (
        weight
        * jnp.sum(masked * (along_x * along_x + along_y * along_y + along_z * along_z), -1)
        / particle_count_field
    )
    thermal_level = (
        motion_squared_half
        - mean_flow_first_axis * mean_flow_first_axis
        - mean_flow_second_axis * mean_flow_second_axis
        - mean_flow_third_axis * mean_flow_third_axis
    ) / 3.0
    relative_speed_first = along_x - mean_flow_first_axis[..., None]
    relative_speed_second = along_y - mean_flow_second_axis[..., None]
    relative_speed_third = along_z - mean_flow_third_axis[..., None]
    maxwell_prefactor = 2.0 * math.pi * thermal_level
    maxwell_target_state = (
        particle_count_field / (maxwell_prefactor * jnp.sqrt(maxwell_prefactor))
    )[..., None] * jnp.exp(
        -(
            relative_speed_first * relative_speed_first
            + relative_speed_second * relative_speed_second
            + relative_speed_third * relative_speed_third
        )
        / (2.0 * thermal_level[..., None])
    )
    forward_x = jnp.maximum(along_x, 0.0)
    backward_x = jnp.minimum(along_x, 0.0)
    forward_y = jnp.maximum(along_y, 0.0)
    backward_y = jnp.minimum(along_y, 0.0)
    transport = forward_x * (distribution - from_lower) + backward_x * (from_upper - distribution)
    transport = (
        transport
        + forward_y * (distribution - from_left)
        + backward_y * (from_right - distribution)
    )
    result = (
        distribution
        - cfl_ratio * transport
        + relax_rate[..., None] * (maxwell_target_state - distribution)
    )
    return jnp.where(valid, result, 0.0)


def grid_points(level):
    return jnp.where(level == 1, NVF, NVC).astype(jnp.int32)


def place_half(half_layer, start, points):
    blank = jnp.zeros((half_layer.shape[0], points), jnp.float32)
    return lax.dynamic_update_slice(blank, half_layer, (jnp.zeros((), jnp.int32), start))


def remap_group(face_tile, source_level, offset_blocks, block_link, remap_values):
    cells_y = face_tile.shape[0]
    local_count = remap_values.shape[1]
    coarse_source = source_level == 0
    values = lax.dynamic_index_in_dim(remap_values, source_level, 0, keepdims=False)
    slot_index = jnp.arange(VBF // 2, dtype=jnp.int32)
    group_size = lax.axis_size("gy")
    every_fine = jnp.arange(VBF, dtype=jnp.int32)
    in_every = jnp.where(coarse_source, block_link[0], every_fine)
    out_every = jnp.where(coarse_source, every_fine, block_link[1])
    own_pieces = face_tile.reshape(cells_y, VBF, BLK)
    outgoing = jnp.take(own_pieces, in_every, axis=1).reshape(cells_y, group_size, local_count, BLK)
    arrived = lax.all_to_all(outgoing, "gy", split_axis=1, concat_axis=0, tiled=True)
    inputs = arrived.reshape(group_size * cells_y, local_count, BLK)
    products = jnp.einsum("rjx,jxy->rjy", inputs, values, preferred_element_type=jnp.float32)
    returned = lax.all_to_all(
        products.astype(jnp.bfloat16), "gy", split_axis=0, concat_axis=1, tiled=True
    ).astype(products.dtype)
    selector = (out_every[:, None] - offset_blocks == slot_index[None, :]).astype(jnp.float32)
    summed = jnp.einsum("rfy,fs->rsy", returned, selector, precision=lax.Precision.HIGHEST)
    return summed.reshape(cells_y, NVF // 2)


def on_device(distribution, relax_rate, block_level, block_link, remap_values):
    cells_x, cells_y, points = distribution.shape
    block_x = lax.axis_index("gx")
    blocks_x = lax.axis_size("gx")
    own_level = block_level[block_x]
    lower_level = block_level[jnp.maximum(block_x - 1, 0)]
    upper_level = block_level[jnp.minimum(block_x + 1, blocks_x - 1)]
    lower_differs = (block_x > 0) & (lower_level != own_level)
    upper_differs = (block_x < blocks_x - 1) & (upper_level != own_level)
    own_points = grid_points(own_level)
    padded = with_halo(distribution.astype(jnp.bfloat16), (("gx", 0), ("gy", 1)), 1).astype(
        distribution.dtype
    )
    lower_raw = padded[0, 1:-1]
    upper_raw = padded[-1, 1:-1]
    face_tile = jnp.where(lower_differs, lower_raw, upper_raw).astype(jnp.bfloat16)
    offset_blocks = jnp.where(lower_differs, own_points // (2 * BLK), 0)
    remapped = remap_group(face_tile, 1 - own_level, offset_blocks, block_link, remap_values)
    lower_ghost = jnp.where(lower_differs, place_half(remapped, own_points // 2, points), lower_raw)
    upper_ghost = jnp.where(
        upper_differs, place_half(remapped, jnp.zeros((), jnp.int32), points), upper_raw
    )
    from_left = padded[1:-1, :-2]
    from_right = padded[1:-1, 2:]
    from_lower = jnp.concatenate([lower_ghost[None], distribution[:-1]], 0)
    from_upper = jnp.concatenate([distribution[1:], upper_ghost[None]], 0)
    return relax_update(
        distribution, relax_rate, own_level, from_lower, from_upper, from_left, from_right
    )


def solution(mesh):
    in_specs = (P("gx", "gy", None), P("gx", "gy"), P(), P(), P(None, "gy", None, None))
    out_specs = P("gx", "gy", None)
    return jax.shard_map(
        on_device, mesh=mesh, in_specs=in_specs, out_specs=out_specs, check_vma=False
    )
```

profile of v0, /device:TPU:2, one launch (start us, length us, event | category | flops | bytes accessed | tf_op | source)
XLA Modules:
  0.0 98.5 jit_solution(1533194137621067974)
XLA Ops:
  0.0 0.0 copy-start
  0.0 1.4 %fusion.52 = (s32[1]{0:T(128)}, s32[1]{0:T(128)}, s32[1]{0:T(128)}) fusion(s32[8]{0:T(128)} %param.7, s32[]{:T(128)S(6)} %select_n.217, s32[]{:T(128)S(6)} %select_n.192, s32[]{:T(128)S(6)} %max.18), kind=kLoop, calls=%fused_computation.97 | loop fusion | bytes 36 | tf_op jit(solution)/shard_map/dynamic_slice | solution.py:136
  2.1 2.5 %fusion.30 = (f32[32768]{0:T(1024)S(1)}, f32[32768]{0:T(1024)S(1)}) fusion(f32[]{:T(128)S(6)} %mul.389, s32[]{:T(128)S(6)} %mul.386, s32[]{:T(128)S(6)} %sign.46, f32[]{:T(128)} %bitcast.1, s32[]{:T(128)S(6)} %select_n.221), kind=kLoop, calls=%fused_computation.51 | loop fusion | flops 655360 | bytes 262164 | tf_op jit(solution)/shard_map/mul | solution.py:39
  4.6 0.0 copy-start.2
  4.6 0.0 copy-start.3
  4.6 5.0 %fusion.34 = (f32[32768]{0:T(1024)S(1)}, f32[32768]{0:T(1024)S(1)}) fusion(s32[]{:T(128)S(6)} %select_n.221, s32[]{:T(128)} %bitcast, s32[]{:T(128)S(6)} %sign.48, f32[]{:T(128)S(6)} %mul.389, f32[]{:T(128)} %bitcast.1, s32[]{:T(128)S(6)} %mul.386, s32[]{:T(128)S(6)} %sign.46), kind=kLoop, calls=%fused_computation.55 | loop fusion | flops 1343488 | bytes 262172 | tf_op jit(solution)/shard_map/mul | solution.py:40
  9.7 0.0 copy-start.4
  9.7 0.0 copy-start.5
  9.7 2.7 %multiply_reduce_fusion.3 = (f32[8]{0:T(128)}, f32[8]{0:T(128)}, f32[8]{0:T(128)}, f32[8]{0:T(128)}, f32[8]{0:T(128)}, /*index=5*/bf16[1,8,32768]{2,1,0:T(8,128)(2,1)S(1)}) fusion(f32[1,8,32768]{2,1,0:T(8,128)} %param.5, f32[32768]{0:T(1024)S(1)} %get-tuple-element.22, pred[32768]{0:T(1024)(128)(4,1)S(1)} %iota_compare_fusion, ...), kind=kLoop, calls=%fused_computation.31 | loop fusion | flops 2883544 | bytes 2130080 | tf_op jit(solution)/shard_map/reduce_sum | solution.py:57
  12.4 0.0 copy-done.2
  12.4 0.0 copy-done.3
  12.4 0.0 copy-done.4
  12.4 0.0 copy-done.5
  12.4 1.9 %collective-permute-start = (bf16[1,8,32768]{2,1,0:T(8,128)(2,1)S(1)}, bf16[1,8,32768]{2,1,0:T(8,128)(2,1)S(1)}, u32[]{:S(2)}, u32[]{:S(2)}) collective-permute-start(bf16[1,8,32768]{2,1,0:T(8,128)(2,1)S(1)} %get-tuple-element.17), channel_id=1, source_target_pairs={{0,4},{4,8},{8,12},{12,16},{16,20},{20,24},{24,28},{1,5},{5,9},{9,... | collective-permute-start | bytes 1572872 | tf_op jit(solution)/shard_map/ppermute | solution.py:28
  14.4 3.6 %collective-permute-start.1 = (bf16[1,8,32768]{2,1,0:T(8,128)(2,1)S(1)}, bf16[1,8,32768]{2,1,0:T(8,128)(2,1)S(1)}, u32[]{:S(2)}, u32[]{:S(2)}) collective-permute-start(bf16[1,8,32768]{2,1,0:T(8,128)(2,1)S(1)} %get-tuple-element.17), channel_id=1, source_target_pairs={{4,0},{8,4},{12,8},{16,12},{20,16},{24,20},{28,24},{5,1},{9,5},{13... | collective-permute-start | bytes 1572872 | tf_op jit(solution)/shard_map/ppermute | solution.py:29
  19.9 0.7 slice_reduce_fusion
  20.6 0.1 squeeze.23
  20.7 0.7 fusion.50
  21.4 1.5 %collective-permute-done = bf16[1,8,32768]{2,1,0:T(8,128)(2,1)S(1)} collective-permute-done((bf16[1,8,32768]{2,1,0:T(8,128)(2,1)S(1)}, bf16[1,8,32768]{2,1,0:T(8,128)(2,1)S(1)}, u32[]{:S(2)}, u32[]{:S(2)}) %collective-permute-start) | collective-permute-done | bytes 524320 | tf_op jit(solution)/shard_map/ppermute | solution.py:28
  22.9 4.6 %collective-permute-done.1 = bf16[1,8,32768]{2,1,0:T(8,128)(2,1)S(1)} collective-permute-done((bf16[1,8,32768]{2,1,0:T(8,128)(2,1)S(1)}, bf16[1,8,32768]{2,1,0:T(8,128)(2,1)S(1)}, u32[]{:S(2)}, u32[]{:S(2)}) %collective-permute-start.1) | collective-permute-done | bytes 524320 | tf_op jit(solution)/shard_map/ppermute | solution.py:29
  27.6 0.5 pad_maximum_fusion.8
  28.1 0.3 copy.29
  28.4 3.5 %collective-permute-start.2 = (bf16[3,1,32768]{2,0,1:T(4,128)(2,1)S(1)}, bf16[3,1,32768]{2,0,1:T(4,128)(2,1)S(1)}, u32[]{:S(2)}, u32[]{:S(2)}) collective-permute-start(bf16[3,1,32768]{2,0,1:T(4,128)(2,1)S(1)} %copy.29), channel_id=1, source_target_pairs={{0,1},{1,2},{2,3},{4,5},{5,6},{6,7},{8,9},{9,10},{10,11},{12,13},{... | collective-permute-start | bytes 589832 | tf_op jit(solution)/shard_map/ppermute | solution.py:28
  31.9 0.3 copy.30
  32.1 1.5 %collective-permute-start.3 = (bf16[3,1,32768]{2,0,1:T(4,128)(2,1)S(1)}, bf16[3,1,32768]{2,0,1:T(4,128)(2,1)S(1)}, u32[]{:S(2)}, u32[]{:S(2)}) collective-permute-start(bf16[3,1,32768]{2,0,1:T(4,128)(2,1)S(1)} %copy.30), channel_id=1, source_target_pairs={{1,0},{2,1},{3,2},{5,4},{6,5},{7,6},{9,8},{10,9},{11,10},{13,12},{... | collective-permute-start | bytes 589832 | tf_op jit(solution)/shard_map/ppermute | solution.py:29
  33.6 4.1 %collective-permute-done.2 = bf16[3,1,32768]{2,0,1:T(4,128)(2,1)S(1)} collective-permute-done((bf16[3,1,32768]{2,0,1:T(4,128)(2,1)S(1)}, bf16[3,1,32768]{2,0,1:T(4,128)(2,1)S(1)}, u32[]{:S(2)}, u32[]{:S(2)}) %collective-permute-start.2) | collective-permute-done | bytes 196640 | tf_op jit(solution)/shard_map/ppermute | solution.py:28
  37.8 0.3 copy.31
  38.1 4.7 %collective-permute-done.3 = bf16[3,1,32768]{2,0,1:T(4,128)(2,1)S(1)} collective-permute-done((bf16[3,1,32768]{2,0,1:T(4,128)(2,1)S(1)}, bf16[3,1,32768]{2,0,1:T(4,128)(2,1)S(1)}, u32[]{:S(2)}, u32[]{:S(2)}) %collective-permute-start.3) | collective-permute-done | bytes 196640 | tf_op jit(solution)/shard_map/ppermute | solution.py:29
  42.8 0.3 copy.32
  43.1 0.0 copy-start.1
  43.1 0.7 copy-done.1
  43.9 1.3 %fusion.20 = bf16[1,8,32768]{2,1,0:T(8,128)(2,1)} fusion(pred[]{:T(512)S(6)} %and.87, bf16[3,1,32768]{2,1,0:T(2,128)(2,1)S(1)} %copy.32, bf16[1,8,32768]{2,1,0:T(8,128)(2,1)S(1)} %collective-permute-done.1, bf16[1,8,32768]{2,1,0:T(8,128)(2,1)S(1)} %get-tuple-element.17, bf16[1,8,32768]{2,1,0:T(8,128)(2,1)S(1)} %collective-permute-done, ...), kind=kLoop, calls=%fused_computation.21 | loop fusion | flops 5767168 | bytes 2490369 | tf_op jit(solution)/shard_map/convert_element_type | solution.py:145
  45.1 1.6 %gather_fusion = bf16[64,8,512]{2,1,0:T(8,128)(2,1)S(1)} fusion(bf16[8,64,512]{2,0,1:T(8,128)(2,1)} %bitcast.120, s32[1024]{0:T(1024)S(1)} %pad_clamp_fusion), kind=kCustom, calls=%fused_computation | custom fusion | bytes 1048832 | tf_op jit(solution)/shard_map/jit(_take)/gather | solution.py:118
  46.7 0.2 copy.33
  46.9 0.1 broadcast_select_fusion
  47.0 0.8 copy.34
  47.9 3.8 %all-to-all-start = ((bf16[8,4,16,512]{3,2,0,1:T(8,128)(2,1)}), bf16[8,4,16,512]{3,2,0,1:T(8,128)(2,1)S(1)}, u32[]{:S(2)}, u32[]{:S(2)}) async-start(bf16[8,4,16,512]{3,2,0,1:T(8,128)(2,1)} %copy.34), calls=%async_computation | async-start | bytes 1048576 | tf_op jit(solution)/shard_map/all_to_all | solution.py:119
  52.3 1.2 %fusion.48 = (f32[8]{0:T(128)S(1)}, f32[8]{0:T(128)S(1)}, f32[8]{0:T(128)S(1)}, f32[8]{0:T(128)S(1)}, f32[8]{0:T(128)}) fusion(f32[8]{0:T(128)} %get-tuple-element.9, f32[]{:T(128)S(6)} %mul.405, f32[8]{0:T(128)} %get-tuple-element.5, f32[8]{0:T(128)} %get-tuple-element.6, f32[8]{0:T(128)} %get-tuple-element.7, f32[8]{0:T(128)} %get-tuple-element.8), kind=kLoop, calls=%fused_computation.86 | loop fusion | flops 144 | bytes 324 | tf_op jit(solution)/shard_map/div | solution.py:71
  53.6 3.3 %broadcast_minimum_fusion = (f32[32768]{0:T(1024)}, f32[32768]{0:T(1024)}) fusion(f32[]{:T(128)S(6)} %mul.389, s32[]{:T(128)S(6)} %select_n.221, s32[]{:T(128)} %bitcast, s32[]{:T(128)S(6)} %sign.48, f32[]{:T(128)} %bitcast.1), kind=kLoop, calls=%fused_computation.72 | loop fusion | flops 622592 | bytes 262164 | tf_op jit(solution)/shard_map/min | solution.py:83
  56.9 9.8 %all-to-all-done = bf16[8,4,16,512]{3,2,0,1:T(8,128)(2,1)S(1)} async-done(((bf16[8,4,16,512]{3,2,0,1:T(8,128)(2,1)}), bf16[8,4,16,512]{3,2,0,1:T(8,128)(2,1)S(1)}, u32[]{:S(2)}, u32[]{:S(2)}) %all-to-all-start) | async-done | bytes 524320 | tf_op jit(solution)/shard_map/all_to_all | solution.py:119
  66.6 4.8 %fusion.6 = bf16[32,16,512]{2,0,1:T(8,128)(2,1)S(1)} fusion(bf16[2,16,512,512]{3,2,1,0:T(8,128)(2,1)} %param.9, s32[]{:T(128)S(6)} %select_n.204, bf16[4,8,1,16,512]{4,3,1,0,2:T(8,128)(2,1)S(1)} %bitcast.115), kind=kOutput, calls=%fused_computation.8 | convolution fusion | flops 268697600 | bytes 9437188 | tf_op jit(solution)/shard_map/rjx,jxy->rjy/dot_general | solution.py:121
  71.5 1.1 %copy.36 = bf16[32,16,512]{2,1,0:T(8,128)(2,1)} copy(bf16[32,16,512]{2,0,1:T(8,128)(2,1)S(1)} %fusion.6) | data formatting | bytes 1048576 | tf_op jit(solution)/shard_map/convert_element_type | solution.py:123
  72.6 3.5 %all-to-all-start.1 = ((bf16[32,16,512]{2,1,0:T(8,128)(2,1)}), bf16[32,16,512]{2,1,0:T(8,128)(2,1)S(1)}, u32[]{:S(2)}, u32[]{:S(2)}) async-start(bf16[32,16,512]{2,1,0:T(8,128)(2,1)} %copy.36), calls=%async_computation.1 | async-start | bytes 1048576 | tf_op jit(solution)/shard_map/all_to_all | solution.py:122
  76.1 0.6 broadcast_multiply_fusion
  77.9 0.7 fusion.49
  78.6 2.0 %broadcast_minimum_fusion.1 = (f32[32768]{0:T(1024)}, f32[32768]{0:T(1024)}) fusion(f32[]{:T(128)S(6)} %mul.389, s32[]{:T(128)S(6)} %mul.386, s32[]{:T(128)S(6)} %sign.46, f32[]{:T(128)} %bitcast.1), kind=kLoop, calls=%fused_computation.74 | loop fusion | flops 425984 | bytes 262160 | tf_op jit(solution)/shard_map/min | solution.py:81
  80.6 9.5 %all-to-all-done.1 = bf16[32,16,512]{2,1,0:T(8,128)(2,1)S(1)} async-done(((bf16[32,16,512]{2,1,0:T(8,128)(2,1)}), bf16[32,16,512]{2,1,0:T(8,128)(2,1)S(1)}, u32[]{:S(2)}, u32[]{:S(2)}) %all-to-all-start.1) | async-done | bytes 524320 | tf_op jit(solution)/shard_map/all_to_all | solution.py:122
  90.1 0.2 convolution_bitcast_fusion
  90.4 0.3 copy.38
  90.7 1.0 %broadcast.628 = f32[8,32768]{1,0:T(8,128)} broadcast(f32[]{:T(128)} %constant.114.clone.1), dimensions={} | broadcast | bytes 1048580 | tf_op jit(solution)/shard_map/broadcast.11
  91.7 1.8 %dynamic_update_slice.6 = f32[8,32768]{1,0:T(8,128)} dynamic-update-slice(f32[8,32768]{1,0:T(8,128)} %broadcast.628, f32[8,16384]{1,0:T(8,128)S(1)} %bitcast.113, s32[]{:T(128)} %constant.105.clone.1, s32[]{:T(128)S(6)} %select_n.215) | dynamic-update-slice | bytes 1048580 | tf_op jit(solution)/shard_map/dynamic_update_slice | solution.py:104
  93.5 0.0 copy-done
  93.5 4.8 %fusion.19 = f32[1,8,32768]{2,1,0:T(8,128)} fusion(f32[1,8,32768]{2,1,0:T(8,128)S(1)} %copy-done, f32[8,32768]{1,0:T(8,128)} %dynamic_update_slice.6, f32[8,16384]{1,0:T(8,128)S(1)} %bitcast.114, bf16[3,1,32768]{2,1,0:T(2,128)(2,1)} %copy-done.1, bf16[3,1,32768]{2,1,0:T(2,128)(2,1)S(1)} %copy.31, bf16[1,8,32768]{2,1,0:T(8,128)(2,1)S(1)} %collective-permute-done.1, ...), kind=kLoop, calls=%fused_computation.20 | loop fusion | flops 18350080 | bytes 6586562 | tf_op jit(solution)/shard_map/jit(_where)/select_n | solution.py:95
  (4 shorter events, 0.1 us)
Async XLA Ops:
  0.0 93.5 %copy-start = (f32[1,8,32768]{2,1,0:T(8,128)S(1)}, f32[1,8,32768]{2,1,0:T(8,128)}, u32[]{:S(2)}) copy-start(f32[1,8,32768]{2,1,0:T(8,128)} %param.5) | copy-start | bytes 3145732
  4.6 7.8 %copy-start.2 = (f32[32768]{0:T(1024)}, f32[32768]{0:T(1024)S(1)}, u32[]{:S(2)}) copy-start(f32[32768]{0:T(1024)S(1)} %get-tuple-element.25) | copy-start | bytes 393220
  4.6 7.8 %copy-start.3 = (f32[32768]{0:T(1024)}, f32[32768]{0:T(1024)S(1)}, u32[]{:S(2)}) copy-start(f32[32768]{0:T(1024)S(1)} %get-tuple-element.26) | copy-start | bytes 393220
  9.7 2.8 %copy-start.4 = (f32[32768]{0:T(1024)}, f32[32768]{0:T(1024)S(1)}, u32[]{:S(2)}) copy-start(f32[32768]{0:T(1024)S(1)} %get-tuple-element.21) | copy-start | bytes 393220
  9.7 2.7 %copy-start.5 = (pred[32768]{0:T(1024)(128)(4,1)}, pred[32768]{0:T(1024)(128)(4,1)S(1)}, u32[]{:S(2)}) copy-start(pred[32768]{0:T(1024)(128)(4,1)S(1)} %iota_compare_fusion) | copy-start | bytes 98308
  12.4 10.5 %collective-permute-start = (bf16[1,8,32768]{2,1,0:T(8,128)(2,1)S(1)}, bf16[1,8,32768]{2,1,0:T(8,128)(2,1)S(1)}, u32[]{:S(2)}, u32[]{:S(2)}) collective-permute-start(bf16[1,8,32768]{2,1,0:T(8,128)(2,1)S(1)} %get-tuple-element.17), channel_id=1, source_target_pairs={{0,4},{4,8},{8,12},{12,16},{16,20},{20,24},{24,28},{1,5},{5,9},{9,... | collective-permute-start | bytes 1572872 | tf_op jit(solution)/shard_map/ppermute | solution.py:28
  14.4 13.2 %collective-permute-start.1 = (bf16[1,8,32768]{2,1,0:T(8,128)(2,1)S(1)}, bf16[1,8,32768]{2,1,0:T(8,128)(2,1)S(1)}, u32[]{:S(2)}, u32[]{:S(2)}) collective-permute-start(bf16[1,8,32768]{2,1,0:T(8,128)(2,1)S(1)} %get-tuple-element.17), channel_id=1, source_target_pairs={{4,0},{8,4},{12,8},{16,12},{20,16},{24,20},{28,24},{5,1},{9,5},{13... | collective-permute-start | bytes 1572872 | tf_op jit(solution)/shard_map/ppermute | solution.py:29
  28.4 9.4 %collective-permute-start.2 = (bf16[3,1,32768]{2,0,1:T(4,128)(2,1)S(1)}, bf16[3,1,32768]{2,0,1:T(4,128)(2,1)S(1)}, u32[]{:S(2)}, u32[]{:S(2)}) collective-permute-start(bf16[3,1,32768]{2,0,1:T(4,128)(2,1)S(1)} %copy.29), channel_id=1, source_target_pairs={{0,1},{1,2},{2,3},{4,5},{5,6},{6,7},{8,9},{9,10},{10,11},{12,13},{... | collective-permute-start | bytes 589832 | tf_op jit(solution)/shard_map/ppermute | solution.py:28
  32.1 10.6 %collective-permute-start.3 = (bf16[3,1,32768]{2,0,1:T(4,128)(2,1)S(1)}, bf16[3,1,32768]{2,0,1:T(4,128)(2,1)S(1)}, u32[]{:S(2)}, u32[]{:S(2)}) collective-permute-start(bf16[3,1,32768]{2,0,1:T(4,128)(2,1)S(1)} %copy.30), channel_id=1, source_target_pairs={{1,0},{2,1},{3,2},{5,4},{6,5},{7,6},{9,8},{10,9},{11,10},{13,12},{... | collective-permute-start | bytes 589832 | tf_op jit(solution)/shard_map/ppermute | solution.py:29
  43.1 0.7 copy-start.1
  47.9 18.8 %all-to-all-start = ((bf16[8,4,16,512]{3,2,0,1:T(8,128)(2,1)}), bf16[8,4,16,512]{3,2,0,1:T(8,128)(2,1)S(1)}, u32[]{:S(2)}, u32[]{:S(2)}) async-start(bf16[8,4,16,512]{3,2,0,1:T(8,128)(2,1)} %copy.34), calls=%async_computation | async-start | bytes 1048576 | tf_op jit(solution)/shard_map/all_to_all | solution.py:119
  72.6 17.5 %all-to-all-start.1 = ((bf16[32,16,512]{2,1,0:T(8,128)(2,1)}), bf16[32,16,512]{2,1,0:T(8,128)(2,1)S(1)}, u32[]{:S(2)}, u32[]{:S(2)}) async-start(bf16[32,16,512]{2,1,0:T(8,128)(2,1)} %copy.36), calls=%async_computation.1 | async-start | bytes 1048576 | tf_op jit(solution)/shard_map/all_to_all | solution.py:122
where the time goes:
time: 99.3 us; the launch traced here: 98.5 us
  waiting for transfers between devices  34.2 us (34%)
  other arithmetic  25.5 us (26%)
  starting transfers between devices  17.8 us (18%)
  local copies, waits for them, and re-layouts  11.1 us (11%)
  matrix products  5.05 us (5%)
  between operations  4.8 us (5%)
    all_to_all x1, waiting for transfers between devices, remap_group(): lax.all_to_all(outgoing, 'gy', split_axis=1, concat_axis=0, tiled=True)  9.78 us
    all_to_all x1, waiting for transfers between devices, remap_group(): lax.all_to_all(products.astype(jnp.bfloat16), 'gy', split_axis=0, concat_...  9.47 us
    ppermute x2, waiting for transfers between devices, with_halo(): after = lax.ppermute(leading, axis, down)  9.29 us
    ppermute x2, waiting for transfers between devices, with_halo(): before = lax.ppermute(last, axis, up)  5.67 us
    ppermute x2, starting transfers between devices, with_halo(): before = lax.ppermute(last, axis, up)  5.42 us
    ppermute x2, starting transfers between devices, with_halo(): after = lax.ppermute(leading, axis, down)  5.11 us
    mul x1, other arithmetic, velocity_tables(): along_y = spacing * ((position // side % side).astype(jnp.float32) - centre)  5.03 us
    dot_general x1, matrix products, remap_group(): jnp.einsum('rjx,jxy->rjy', inputs, values, preferred_element_type=jnp.flo...  4.84 us
  transfers between devices with their start and end apart: 6, of which 6 were waited for; matrix products, arithmetic and copies ran while one was open for 10% of the time, Pallas kernels for 0%

commit v1 on v0

v1 whole, which is shorter than its diff:
```python
import functools
import math

import jax
import jax.numpy as jnp
from jax import lax
from jax.experimental import pallas as pl
from jax.experimental.pallas import tpu as pltpu
from jax.sharding import PartitionSpec as P

SC = 16
SF = 32
BLK = 512
NVC = 4096
NVF = 32768
VBC = NVC // BLK
VBF = NVF // BLK
HALF_F = VBF // 2
HALF_C = VBC // 2

cfl_ratio = 0.03
spacing_coarse = 0.5
spacing_fine = 0.4

BOTH = ("gx", "gy")
SMEM = pl.BlockSpec(memory_space=pltpu.SMEM)
VMEM = pl.BlockSpec(memory_space=pltpu.VMEM)
ANY = pl.BlockSpec(memory_space=pl.ANY)
F32 = jnp.float32
BF16 = jnp.bfloat16


def place(level_ref):
    block = lax.axis_index("gx")
    own = level_ref[block]
    lower = level_ref[jnp.maximum(block - 1, 0)]
    upper = level_ref[jnp.minimum(block + 1, level_ref.shape[0] - 1)]
    return block, own, lower != own, upper != own


def block_at(ref, index):
    return ref[:, pl.ds(pl.multiple_of(index * BLK, BLK), BLK)]


def prepare_kernel(
    level_ref, link_ref, cells_ref, even_ref, odd_ref, ahead_ref, back_ref, index_ref, row_ref
):
    block, own, lower_differs, upper_differs = place(level_ref)
    fine = own == 1
    cells_y = cells_ref.shape[0]

    def fill(target_ref, going_up):
        differs = jnp.where(going_up, upper_differs, lower_differs)
        gathers = differs & fine

        @pl.when(gathers)
        def _():
            def look(f, count):
                index_ref[count] = f
                hit = (link_ref[1, f] >= HALF_C) == going_up
                return count + hit.astype(jnp.int32)

            lax.fori_loop(0, VBF, look, jnp.int32(0), unroll=4)

        @pl.when(jnp.logical_not(gathers))
        def _():
            plain = going_up & jnp.logical_not(differs)
            start = jnp.where(plain, jnp.where(fine, HALF_F, HALF_C), 0)

            def number(j, carry):
                index_ref[j] = start + j
                return carry

            lax.fori_loop(0, HALF_F, number, 0, unroll=4)

        def copy(j, carry):
            target_ref[j] = block_at(cells_ref, index_ref[j]).astype(BF16)
            return carry

        @pl.when(fine)
        def _():
            lax.fori_loop(0, HALF_F, copy, 0, unroll=4)

        @pl.when(jnp.logical_not(fine))
        def _():
            lax.fori_loop(0, VBC, copy, 0, unroll=4)

    on_even = block % 2 == 0
    fill(odd_ref, jnp.logical_not(on_even))
    fill(even_ref, on_even)

    def rows(target_ref, row, parity):
        @pl.when(fine)
        def _():
            for i in range(HALF_F):
                row_ref[i : i + 1, :] = cells_ref[
                    row : row + 1, (2 * i + parity) * BLK : (2 * i + parity + 1) * BLK
                ]

        @pl.when(jnp.logical_not(fine))
        def _():
            for i in range(VBC):
                row_ref[i : i + 1, :] = cells_ref[row : row + 1, i * BLK : (i + 1) * BLK]

        target_ref[...] = row_ref[...].astype(BF16)

    rows(ahead_ref, cells_y - 1, 1)
    rows(back_ref, 0, 0)


def prepare(levels, links, cells):
    half = jax.ShapeDtypeStruct((HALF_F, cells.shape[0], BLK), BF16)
    row = jax.ShapeDtypeStruct((HALF_F, BLK), BF16)
    return pl.pallas_call(
        prepare_kernel,
        name="prepare",
        out_shape=(half, half, row, row),
        in_specs=[SMEM, SMEM, VMEM],
        out_specs=(VMEM,) * 4,
        scratch_shapes=[pltpu.SMEM((VBF + 1,), jnp.int32), pltpu.VMEM((HALF_F, BLK), F32)],
        cost_estimate=pl.CostEstimate(flops=10**6, bytes_accessed=2 * 10**6, transcendentals=0),
        compiler_params=pltpu.CompilerParams(vmem_limit_bytes=8 << 20),
    )(levels, links, cells)


def relax_kernel(level_ref, rate_ref, cells_ref, left_ref, right_ref, out_ref, side_ref):
    _, own, _, _ = place(level_ref)
    rows_n = cells_ref.shape[0]

    def run(side, spacing):
        width = side * side
        mid = width // 2
        centre = (side - 1) * 0.5
        lane = lax.broadcasted_iota(jnp.int32, (rows_n, width), 1)
        along_y = spacing * ((lane // side).astype(F32) - centre)
        along_z = spacing * ((lane % side).astype(F32) - centre)

        def plane_at(i):
            return cells_ref[:, pl.ds(pl.multiple_of(i * width, width), width)]

        def speed_at(i):
            return spacing * (lax.convert_element_type(i, F32) - centre)

        def gather(i, sums):
            total, first, second = sums
            plane = plane_at(i)
            speed = speed_at(i)
            return total + plane, first + plane * speed, second + plane * (speed * speed)

        zero = jnp.zeros((rows_n, width), F32)
        total, first, second = lax.fori_loop(0, side, gather, (zero, zero, zero), unroll=4)

        def over(value):
            return jnp.broadcast_to(jnp.sum(value, axis=1, keepdims=True), (rows_n, 128))

        weight = spacing * spacing * spacing
        density = weight * over(total)
        scale = weight / density
        mean_x = scale * over(first)
        mean_y = scale * over(total * along_y)
        mean_z = scale * over(total * along_z)
        square = scale * over(second + total * (along_y * along_y + along_z * along_z))
        heat = (square - mean_x * mean_x - mean_y * mean_y - mean_z * mean_z) / 3.0
        row = lax.broadcasted_iota(jnp.int32, (rows_n, 128), 0)
        rate = jnp.zeros((rows_n, 128), F32)
        for r in range(rows_n):
            rate = jnp.where(row == r, rate_ref[0, r], rate)
        spread = 2.0 * math.pi * heat
        peak = rate * density / (spread * jnp.sqrt(spread))
        inverse = -0.5 / heat

        def wide(value):
            return jnp.concatenate([value] * (width // 128), axis=1)

        off_y = along_y - wide(mean_y)
        off_z = along_z - wide(mean_z)
        across = wide(peak) * jnp.exp((off_y * off_y + off_z * off_z) * wide(inverse))
        drift = cfl_ratio * jnp.abs(along_y)
        keep = (1.0 - wide(rate)) - drift
        wide_row = lax.broadcasted_iota(jnp.int32, (rows_n, mid), 0)

        def update(i, carry):
            plane = plane_at(i)
            speed = speed_at(i)
            off_x = speed - mean_x
            along = wide(jnp.exp(off_x * off_x * inverse))
            if side == SF:
                right = side_ref[1, pl.ds(i, 1), :]
                left = side_ref[0, pl.ds(i, 1), :]
            else:
                slot, offset = i // 2, (i % 2) * width
                right = side_ref[1, slot : slot + 1, offset : offset + mid]
                left = side_ref[0, slot : slot + 1, offset + mid : offset + width]
            low, high = plane[:, :mid], plane[:, mid:]
            beyond = jnp.where(wide_row == rows_n - 1, right, pltpu.roll(low, rows_n - 1, 0))
            before = jnp.where(wide_row == 0, left, pltpu.roll(high, 1, 0))
            beside = jnp.concatenate([beyond, before], axis=1)
            factor = keep - cfl_ratio * jnp.abs(speed)
            out_ref[:, pl.ds(pl.multiple_of(i * width, width), width)] = (
                plane * factor + drift * beside + along * across
            )
            return carry

        if side == SF:
            lax.fori_loop(0, side, update, 0, unroll=4)
        else:
            for i in range(side):
                update(i, 0)

    side_ref[0] = left_ref[...].astype(F32)
    side_ref[1] = right_ref[...].astype(F32)

    @pl.when(own == 1)
    def _():
        run(SF, spacing_fine)

    @pl.when(own != 1)
    def _():
        run(SC, spacing_coarse)


def relax(levels, rate, cells, left, right):
    return pl.pallas_call(
        relax_kernel,
        name="relax",
        out_shape=jax.ShapeDtypeStruct(cells.shape, F32),
        in_specs=[SMEM, SMEM, VMEM, VMEM, VMEM],
        out_specs=VMEM,
        scratch_shapes=[pltpu.VMEM((2, HALF_F, BLK), F32)],
        cost_estimate=pl.CostEstimate(flops=10**7, bytes_accessed=4 * 10**6, transcendentals=10**5),
        compiler_params=pltpu.CompilerParams(vmem_limit_bytes=16 << 20),
    )(levels, rate, cells, left, right)


def pieces_kernel(group, level_ref, link_ref, even_ref, odd_ref, *out_refs):
    block, own, lower_differs, _ = place(level_ref)
    me = lax.axis_index("gy")
    local = VBF // group
    use_even = (block % 2 == 0) != lower_differs

    def count(f, starts):
        hit = ((link_ref[1, f] >= HALF_C) == lower_differs).astype(jnp.int32)
        return starts + hit

    def fill(source_ref):
        for s, out_ref in enumerate(out_refs):
            holder = lax.rem(me + s, group)
            start = lax.fori_loop(0, holder * local, count, jnp.int32(0))
            for j in range(local):
                out_ref[j] = source_ref[jnp.minimum(start + j, HALF_F - 1)]

    @pl.when(use_even)
    def _():
        fill(even_ref)

    @pl.when(jnp.logical_not(use_even))
    def _():
        fill(odd_ref)


def pieces(levels, links, even, odd, group):
    piece = jax.ShapeDtypeStruct((VBF // group,) + even.shape[1:], BF16)
    return pl.pallas_call(
        functools.partial(pieces_kernel, group),
        name="pieces",
        out_shape=(piece,) * group,
        in_specs=[SMEM, SMEM, VMEM, VMEM],
        out_specs=(VMEM,) * group,
        cost_estimate=pl.CostEstimate(flops=10**5, bytes_accessed=10**6, transcendentals=0),
        compiler_params=pltpu.CompilerParams(vmem_limit_bytes=8 << 20),
    )(levels, links, even, odd)


def coarse_kernel(group, level_ref, even_ref, odd_ref, out_ref):
    block, own, lower_differs, _ = place(level_ref)
    use_even = (block % 2 == 0) != lower_differs

    @pl.when(use_even)
    def _():
        out_ref[...] = even_ref[0:VBC]

    @pl.when(jnp.logical_not(use_even))
    def _():
        out_ref[...] = odd_ref[0:VBC]


def coarse_piece(levels, even, odd, group):
    return pl.pallas_call(
        functools.partial(coarse_kernel, group),
        name="coarse_piece",
        out_shape=jax.ShapeDtypeStruct((VBC,) + even.shape[1:], BF16),
        in_specs=[SMEM, VMEM, VMEM],
        out_specs=VMEM,
        cost_estimate=pl.CostEstimate(flops=10**5, bytes_accessed=10**6, transcendentals=0),
        compiler_params=pltpu.CompilerParams(vmem_limit_bytes=8 << 20),
    )(levels, even, odd)


def stacked(refs, index):
    return jnp.concatenate([ref[index].astype(F32) for ref in refs], axis=0).astype(BF16)


def to_coarse_kernel(group, level_ref, link_ref, values_ref, *refs):
    in_refs, out_refs = refs[:group], refs[group : 2 * group]
    held_ref, sum_ref, sems = refs[2 * group :]
    _, _, lower_differs, _ = place(level_ref)
    local = values_ref.shape[1]
    cells_y = in_refs[0].shape[1]
    first = lax.axis_index("gy") * local
    offset = jnp.where(lower_differs, HALF_C, 0)

    def copy(j):
        return pltpu.make_async_copy(values_ref.at[1, j], held_ref.at[j], sems.at[j])

    targets = [link_ref[1, first + j] - offset for j in range(local)]
    needed = [(t >= 0) & (t < HALF_C) for t in targets]
    for j in range(local):

        @pl.when(needed[j])
        def _(j=j):
            copy(j).start()

    sum_ref[...] = jnp.zeros_like(sum_ref)
    slot = jnp.int32(0)
    for j in range(local):

        @pl.when(needed[j])
        def _(j=j, slot=slot):
            copy(j).wait()
            sum_ref[targets[j]] += jnp.dot(
                stacked(in_refs, slot), held_ref[j], preferred_element_type=F32
            )

        slot = slot + needed[j].astype(jnp.int32)
    for s, out_ref in enumerate(out_refs):
        out_ref[...] = sum_ref[:, s * cells_y : (s + 1) * cells_y, :].astype(BF16)


def to_fine_kernel(group, level_ref, link_ref, values_ref, *refs):
    in_refs, out_refs = refs[:group], refs[group : 2 * group]
    held_ref, sems = refs[2 * group :]
    _, _, lower_differs, _ = place(level_ref)
    local = values_ref.shape[1]
    cells_y = in_refs[0].shape[1]
    first = lax.axis_index("gy") * local
    active = (first >= HALF_F) == lower_differs

    @pl.when(active)
    def _():
        def copy(j):
            return pltpu.make_async_copy(values_ref.at[0, j], held_ref.at[j], sems.at[j])

        for j in range(local):
            copy(j).start()
        for j in range(local):
            copy(j).wait()
            product = jnp.dot(
                stacked(in_refs, link_ref[0, first + j]),
                held_ref[j],
                preferred_element_type=F32,
            ).astype(BF16)
            for s, out_ref in enumerate(out_refs):
                out_ref[j] = product[s * cells_y : (s + 1) * cells_y, :]


def multiply(kernel, levels, links, values, arrived, slots, scratch):
    group = len(arrived)
    local = values.shape[1]
    out = jax.ShapeDtypeStruct((slots,) + arrived[0].shape[1:], BF16)
    return pl.pallas_call(
        functools.partial(kernel, group),
        name=kernel.__name__,
        out_shape=(out,) * group,
        in_specs=[SMEM, SMEM, ANY] + [VMEM] * group,
        out_specs=(VMEM,) * group,
        scratch_shapes=[pltpu.VMEM((local, BLK, BLK), BF16)]
        + scratch
        + [pltpu.SemaphoreType.DMA((local,))],
        cost_estimate=pl.CostEstimate(
            flops=2 * local * 32 * BLK * BLK, bytes_accessed=2 * local * BLK * BLK, transcendentals=0
        ),
        compiler_params=pltpu.CompilerParams(vmem_limit_bytes=24 << 20),
    )(levels, links, values, *arrived)


def finish_kernel(role, group, level_ref, base_ref, even_ref, odd_ref, *refs):
    in_refs, out_ref = refs[:-1], refs[-1]
    block, own, lower_differs, upper_differs = place(level_ref)
    on_even = block % 2 == 0
    me = lax.axis_index("gy")

    def add(index, ghost, side, spacing):
        per = (side * side) // 128
        centre = (side - 1) * 0.5
        for c in range(BLK // 128):
            plane = (index * (BLK // 128) + c) // per
            speed = cfl_ratio * spacing * jnp.abs(lax.convert_element_type(plane, F32) - centre)
            at = pl.ds(pl.multiple_of(index * BLK + c * 128, 128), 128)
            out_ref[:, at] = base_ref[:, at] + speed * ghost[:, c * 128 : (c + 1) * 128]

    def plain(upward, count, side, spacing):
        def step(j, carry):
            a, b = even_ref[j], odd_ref[j]
            take_even = on_even == upward
            ghost = jnp.where(take_even, a.astype(F32), b.astype(F32))
            add(j if upward else count + j, ghost, side, spacing)
            return carry

        lax.fori_loop(0, count, step, 0, unroll=4)

    def halves(count, side, spacing, remapped):
        for upward, differs in ((True, upper_differs), (False, lower_differs)):
            if remapped is None:
                plain(upward, count, side, spacing)
            else:
                pl.when(jnp.logical_not(differs))(
                    functools.partial(plain, upward, count, side, spacing)
                )
                pl.when(differs)(functools.partial(remapped, upward))

    def from_fine(upward):
        for o in range(HALF_C):
            ghost = in_refs[0][o].astype(F32)
            for ref in in_refs[1:]:
                ghost = ghost + ref[o].astype(F32)
            add(o if upward else HALF_C + o, ghost, SC, spacing_coarse)

    def from_coarse(upward):
        for s, ref in enumerate(in_refs):
            local = ref.shape[0]
            first = lax.rem(me + s, group) * local

            @pl.when((first < HALF_F) == upward)
            def _(ref=ref, first=first, local=local):
                def step(j, carry):
                    add(first + j, ref[j].astype(F32), SF, spacing_fine)
                    return carry

                lax.fori_loop(0, local, step, 0, unroll=4)

    def fine():
        halves(HALF_F, SF, spacing_fine, None if role == 0 else from_coarse)

    def coarse():
        out_ref[:, NVC:] = jnp.zeros((out_ref.shape[0], NVF - NVC), F32)
        halves(HALF_C, SC, spacing_coarse, None if role == 0 else from_fine)

    if role != 1:
        pl.when(own == 1)(fine) if role == 0 else fine()
    if role != 2:
        pl.when(own != 1)(coarse) if role == 0 else coarse()


def finish(role, group, levels, base, even, odd, arrived):
    return pl.pallas_call(
        functools.partial(finish_kernel, role, group),
        name="finish",
        out_shape=jax.ShapeDtypeStruct(base.shape, F32),
        in_specs=[SMEM, VMEM, VMEM, VMEM] + [VMEM] * len(arrived),
        out_specs=VMEM,
        cost_estimate=pl.CostEstimate(flops=10**6, bytes_accessed=3 * 10**6, transcendentals=0),
        compiler_params=pltpu.CompilerParams(vmem_limit_bytes=16 << 20),
    )(levels, base, even, odd, *arrived)


def on_device(distribution, relax_rate, block_level, block_link, remap_values):
    blocks, group = lax.axis_size("gx"), lax.axis_size("gy")
    cells_y = distribution.shape[1]
    cells = distribution[0]

    def partners(parity):
        pairs = []
        for low in range(parity, blocks - 1, 2):
            for y in range(group):
                here, there = low * group + y, (low + 1) * group + y
                pairs += [(here, there), (there, here)]
        return pairs

    def shift(value, by):
        return lax.ppermute(value, "gy", [(i, (i + by) % group) for i in range(group)])

    block = lax.axis_index("gx")
    own = block_level[block]
    lower = block_level[jnp.maximum(block - 1, 0)]
    upper = block_level[jnp.minimum(block + 1, blocks - 1)]
    role = jnp.where((lower != own) | (upper != own), 1 + own, 0)

    even, odd, ahead, back = prepare(block_level, block_link, cells)
    odd = lax.ppermute(odd, BOTH, partners(1))
    even = lax.ppermute(even, BOTH, partners(0))

    def beside(ahead, back):
        left = lax.ppermute(ahead, "gy", [(i, i + 1) for i in range(group - 1)])
        right = lax.ppermute(back, "gy", [(i + 1, i) for i in range(group - 1)])
        return relax(block_level, relax_rate, cells, left, right)

    def around(outgoing, by):
        return [outgoing[0]] + [shift(outgoing[s], by * s) for s in range(1, group)]

    def alone(even, odd, ahead, back):
        base = beside(ahead, back)
        return finish(0, group, block_level, base, even, odd, ())

    def to_coarse(even, odd, ahead, back):
        arrived = around(pieces(block_level, block_link, even, odd, group), 1)
        sums = pltpu.VMEM((HALF_C, group * cells_y, BLK), F32)
        made = multiply(
            to_coarse_kernel, block_level, block_link, remap_values, arrived, HALF_C, [sums]
        )
        arrived = around(made, -1)
        base = beside(ahead, back)
        return finish(1, group, block_level, base, even, odd, arrived)

    def to_fine(even, odd, ahead, back):
        piece = coarse_piece(block_level, even, odd, group)
        arrived = around([piece] * group, 1)
        local = remap_values.shape[1]
        made = multiply(to_fine_kernel, block_level, block_link, remap_values, arrived, local, [])
        arrived = around(made, -1)
        base = beside(ahead, back)
        return finish(2, group, block_level, base, even, odd, arrived)

    updated = lax.switch(role, [alone, to_coarse, to_fine], even, odd, ahead, back)
    return updated[None]


def solution(mesh):
    in_specs = (P("gx", "gy", None), P("gx", "gy"), P(), P(), P(None, "gy", None, None))
    out_specs = P("gx", "gy", None)
    return jax.shard_map(
        on_device, mesh=mesh, in_specs=in_specs, out_specs=out_specs, check_vma=False
    )
```

time: 99.3 us -> 46.5 us (0.47)
  other arithmetic: 25.5 us -> 0 us
  waiting for transfers between devices: 34.2 us -> 15.1 us
  local copies, waits for them, and re-layouts: 11.1 us -> 2.4 us
  Pallas kernels: 0 us -> 7.63 us
  matrix products: 5.05 us -> 0 us
  between operations: 4.8 us -> 3.06 us
    all_to_all x2 -> x0, waiting for transfers between devices: 19.2 us -> none  [the longest x1 9.78 us: remap_group(): lax.all_to_all(outgoing, 'gy', split_axis=1, concat_axis=0, tiled=True)]
    mul x3 -> x0, other arithmetic: 8.13 us -> none  [the longest x1 5.03 us: velocity_tables(): along_y = spacing * ((position // side % side).astype(jnp.float32) - centre)]
    pallas_call x0 -> x5, Pallas kernels: none -> 7.63 us  [the longest x1 2.61 us: finish(): pl.pallas_call(functools.partial(finish_kernel, role, group), name='finis...]
    all_to_all x2 -> x0, starting transfers between devices: 7.32 us -> none  [the longest x1 3.85 us: remap_group(): lax.all_to_all(outgoing, 'gy', split_axis=1, concat_axis=0, tiled=True)]
    ppermute x4 -> x10, starting transfers between devices: 10.5 us -> 17.8 us  [the longest x6 12.6 us: shift(): lax.ppermute(value, 'gy', [(i, (i + by) % group) for i in range(group)])]
    select_n x3 -> x0, other arithmetic: 5.63 us -> none  [the longest x1 4.83 us: relax_update(): return jnp.where(valid, result, 0.0)]
    min x2 -> x0, other arithmetic: 5.31 us -> none  [the longest x1 3.3 us: relax_update(): backward_y = jnp.minimum(along_y, 0.0)]
    dot_general x2 -> x0, matrix products: 5.05 us -> none  [the longest x1 4.84 us: remap_group(): jnp.einsum('rjx,jxy->rjy', inputs, values, preferred_element_type=jnp.flo...]
  transfers between devices with their start and end apart: 6 -> 10, of which waited for: 6 -> 5; matrix products, arithmetic and copies ran while one was open for 10% -> 3% of each run, Pallas kernels for 0% -> 3%
where the time goes in v1:
time: 46.5 us; the launch traced here: 46.1 us
  starting transfers between devices  17.8 us (38%)
  waiting for transfers between devices  15.1 us (32%)
  Pallas kernels  7.63 us (16%)
  between operations  3.06 us (7%)
  local copies, waits for them, and re-layouts  2.4 us (5%)
    ppermute x6, starting transfers between devices, shift(): lax.ppermute(value, 'gy', [(i, (i + by) % group) for i in range(group)])  12.6 us
    ppermute x6, waiting for transfers between devices, shift(): lax.ppermute(value, 'gy', [(i, (i + by) % group) for i in range(group)])  6.77 us
    ppermute x1, waiting for transfers between devices, beside(): right = lax.ppermute(back, 'gy', [(i + 1, i) for i in range(group - 1)])  3.63 us
    ppermute x1, waiting for transfers between devices, beside(): left = lax.ppermute(ahead, 'gy', [(i, i + 1) for i in range(group - 1)])  2.79 us
    pallas_call x1, Pallas kernels, finish(): pl.pallas_call(functools.partial(finish_kernel, role, group), name='finis...  2.61 us
    pallas_call x1, Pallas kernels, prepare(): pl.pallas_call(prepare_kernel, name='prepare', out_shape=(half, half, row...  1.98 us
    ppermute x1, starting transfers between devices, on_device(): odd = lax.ppermute(odd, BOTH, partners(1))  1.92 us
    ppermute x1, starting transfers between devices, beside(): left = lax.ppermute(ahead, 'gy', [(i, i + 1) for i in range(group - 1)])  1.9 us
  transfers between devices with their start and end apart: 10, of which 5 were waited for; matrix products, arithmetic and copies ran while one was open for 3% of the time, Pallas kernels for 3%

profile of v1, /device:TPU:2, one launch (start us, length us, event | category | flops | bytes accessed | tf_op | source)
XLA Modules:
  0.0 46.1 jit_solution(12579558245638360178)
XLA Ops:
  0.0 2.0 %prepare.1 = (bf16[32,8,512]{2,1,0:T(8,128)(2,1)S(1)}, bf16[32,8,512]{2,1,0:T(8,128)(2,1)S(1)}, bf16[32,512]{1,0:T(8,128)(2,1)S(1)}, bf16[32,512]{1,0:T(8,128)(2,1)S(1)}) custom-call(s32[8]{0:T(128)} %level_ref.1, s32[2,64]{1,0:T(2,128)} %link_ref.1, f32[8,32768]{1,0:T(8,128)} %bitcast.5), custom_call_target="tpu_custom_call" | custom-call | flops 1000000 | bytes 2000000 | tf_op jit(solution)/shard_map/prepare/pallas_call | solution.py:114
  2.0 0.1 collective-permute-start.18
  2.1 1.9 %collective-permute-start.19 = (bf16[32,8,512]{2,1,0:T(8,128)(2,1)S(1)}, bf16[32,8,512]{2,1,0:T(8,128)(2,1)S(1)}, u32[]{:S(2)}, u32[]{:S(2)}) collective-permute-start(bf16[32,8,512]{2,1,0:T(8,128)(2,1)S(1)} %get-tuple-element.104), channel_id=1, source_target_pairs={{4,8},{8,4},{5,9},{9,5},{6,10},{10,6},{7,11},{11,7},{12,16},{16,12... | collective-permute-start | bytes 786440 | tf_op jit(solution)/shard_map/ppermute | solution.py:489
  4.0 1.4 %fusion = (s32[1]{0:T(128)}, s32[1]{0:T(128)}, s32[1]{0:T(128)}) fusion(s32[8]{0:T(128)} %level_ref.1, s32[]{:T(128)S(6)} %select_n.13, s32[]{:T(128)S(6)} %select_n.12, s32[]{:T(128)S(6)} %max.3), kind=kLoop, calls=%fused_computation | loop fusion | bytes 36 | tf_op jit(solution)/shard_map/dynamic_slice | solution.py:485
  8.4 0.0 collective-permute-done.18
  8.4 1.9 %collective-permute-done.19 = bf16[32,8,512]{2,1,0:T(8,128)(2,1)S(1)} collective-permute-done((bf16[32,8,512]{2,1,0:T(8,128)(2,1)S(1)}, bf16[32,8,512]{2,1,0:T(8,128)(2,1)S(1)}, u32[]{:S(2)}, u32[]{:S(2)}) %collective-permute-start.19) | collective-permute-done | bytes 262176 | tf_op jit(solution)/shard_map/ppermute | solution.py:489
  10.3 34.8 %conditional.1 = (f32[1,8,32768]{2,1,0:T(8,128)S(1)}) conditional(s32[]{:T(128)} %bitcast.3, (bf16[32,512]{1,0:T(8,128)(2,1)S(1)}, bf16[32,512]{1,0:T(8,128)(2,1)S(1)}, s32[8]{0:T(128)}, f32[1,8]{1,0:T(1,128)}, f32[8,32768]{1,0:T(8,128)}, /*index=5*/bf16[32,8,512]{2,1,0:T(8,128)(2,1)S(1)}, ...), branch_computations={%region_0.1_spmd, %region_1.2_spmd, %region_2.3_spmd} | conditional | flops 279535456 | bytes 23205020 | solution.py:523
  10.3 0.0 copy-start.1
  10.3 0.0 copy-start.4
  10.3 0.0 copy-start.6
  10.3 0.8 %coarse_piece.1.refs_0_ = bf16[8,8,512]{2,1,0:T(8,128)(2,1)S(1)} custom-call(s32[8]{0:T(128)} %get-tuple-element.84.level_ref, bf16[32,8,512]{2,1,0:T(8,128)(2,1)S(1)} %get-tuple-element.89.even_ref, bf16[32,8,512]{2,1,0:T(8,128)(2,1)S(1)} %get-tuple-element.90.odd_ref), custom_call_target="tpu_custom_call" | custom-call | flops 100000 | bytes 1000000 | tf_op jit(solution)/shard_map/cond/branch_2_fun/coarse_piece/pallas_call | solution.py:288
  11.2 3.8 %collective-permute-start.14 = (bf16[8,8,512]{2,1,0:T(8,128)(2,1)S(1)}, bf16[8,8,512]{2,1,0:T(8,128)(2,1)S(1)}, u32[]{:S(2)}, u32[]{:S(2)}) collective-permute-start(bf16[8,8,512]{2,1,0:T(8,128)(2,1)S(1)} %coarse_piece.1.refs_0_), channel_id=1, source_target_pairs={{0,3},{1,0},{2,1},{3,2},{4,7},{5,4},{6,5},{7,6},{8,11},{9,8},{10,9... | collective-permute-start | bytes 196616 | tf_op jit(solution)/shard_map/cond/branch_2_fun/ppermute | solution.py:480
  15.0 0.0 collective-permute-start.13
  15.0 1.0 %collective-permute-start.12 = (bf16[8,8,512]{2,1,0:T(8,128)(2,1)S(1)}, bf16[8,8,512]{2,1,0:T(8,128)(2,1)S(1)}, u32[]{:S(2)}, u32[]{:S(2)}) collective-permute-start(bf16[8,8,512]{2,1,0:T(8,128)(2,1)S(1)} %coarse_piece.1.refs_0_), channel_id=1, source_target_pairs={{0,1},{1,2},{2,3},{3,0},{4,5},{5,6},{6,7},{7,4},{8,9},{9,10},{10,1... | collective-permute-start | bytes 196616 | tf_op jit(solution)/shard_map/cond/branch_2_fun/ppermute | solution.py:480
  16.0 0.9 %collective-permute-done.14.refs_3_ = bf16[8,8,512]{2,1,0:T(8,128)(2,1)S(1)} collective-permute-done((bf16[8,8,512]{2,1,0:T(8,128)(2,1)S(1)}, bf16[8,8,512]{2,1,0:T(8,128)(2,1)S(1)}, u32[]{:S(2)}, u32[]{:S(2)}) %collective-permute-start.14) | collective-permute-done | bytes 65568 | tf_op jit(solution)/shard_map/cond/branch_2_fun/ppermute | solution.py:480
  16.9 5.9 %collective-permute-done.13.refs_2_ = bf16[8,8,512]{2,1,0:T(8,128)(2,1)S(1)} collective-permute-done((bf16[8,8,512]{2,1,0:T(8,128)(2,1)S(1)}, bf16[8,8,512]{2,1,0:T(8,128)(2,1)S(1)}, u32[]{:S(2)}, u32[]{:S(2)}) %collective-permute-start.13) | collective-permute-done | bytes 65568 | tf_op jit(solution)/shard_map/cond/branch_2_fun/ppermute | solution.py:480
  22.8 0.0 collective-permute-done.12.refs_1_
  22.8 0.9 %to_fine_kernel.1 = (bf16[16,8,512]{2,1,0:T(8,128)(2,1)S(1)}, bf16[16,8,512]{2,1,0:T(8,128)(2,1)S(1)}, bf16[16,8,512]{2,1,0:T(8,128)(2,1)S(1)}, bf16[16,8,512]{2,1,0:T(8,128)(2,1)S(1)}) custom-call(s32[8]{0:T(128)} %get-tuple-element.84.level_ref, s32[2,64]{1,0:T(2,128)} %get-tuple-element.91.link_ref, ...), custom_call_target="tpu_custom_call" | custom-call | flops 268435456 | bytes 8388608 | tf_op jit(solution)/shard_map/cond/branch_2_fun/to_fine_kernel/pallas_call | solution.py:370
  23.6 3.6 %collective-permute-start.15 = (bf16[16,8,512]{2,1,0:T(8,128)(2,1)S(1)}, bf16[16,8,512]{2,1,0:T(8,128)(2,1)S(1)}, u32[]{:S(2)}, u32[]{:S(2)}) collective-permute-start(bf16[16,8,512]{2,1,0:T(8,128)(2,1)S(1)} %get-tuple-element.94), channel_id=1, source_target_pairs={{0,3},{1,0},{2,1},{3,2},{4,7},{5,4},{6,5},{7,6},{8,11},{9,8},{10,9... | collective-permute-start | bytes 393224 | tf_op jit(solution)/shard_map/cond/branch_2_fun/ppermute | solution.py:480
  27.3 2.2 %collective-permute-start.16 = (bf16[16,8,512]{2,1,0:T(8,128)(2,1)S(1)}, bf16[16,8,512]{2,1,0:T(8,128)(2,1)S(1)}, u32[]{:S(2)}, u32[]{:S(2)}) collective-permute-start(bf16[16,8,512]{2,1,0:T(8,128)(2,1)S(1)} %get-tuple-element.95), channel_id=1, source_target_pairs={{0,2},{1,3},{2,0},{3,1},{4,6},{5,7},{6,4},{7,5},{8,10},{9,11},{10,... | collective-permute-start | bytes 393224 | tf_op jit(solution)/shard_map/cond/branch_2_fun/ppermute | solution.py:480
  29.5 1.9 %collective-permute-start.17 = (bf16[16,8,512]{2,1,0:T(8,128)(2,1)S(1)}, bf16[16,8,512]{2,1,0:T(8,128)(2,1)S(1)}, u32[]{:S(2)}, u32[]{:S(2)}) collective-permute-start(bf16[16,8,512]{2,1,0:T(8,128)(2,1)S(1)} %get-tuple-element.96), channel_id=1, source_target_pairs={{0,1},{1,2},{2,3},{3,0},{4,5},{5,6},{6,7},{7,4},{8,9},{9,10},{10,1... | collective-permute-start | bytes 393224 | tf_op jit(solution)/shard_map/cond/branch_2_fun/ppermute | solution.py:480
  31.4 1.9 %collective-permute-start.10 = (bf16[32,512]{1,0:T(8,128)(2,1)S(1)}, bf16[32,512]{1,0:T(8,128)(2,1)S(1)}, u32[]{:S(2)}, u32[]{:S(2)}) collective-permute-start(bf16[32,512]{1,0:T(8,128)(2,1)S(1)} %get-tuple-element.87), channel_id=1, source_target_pairs={{0,1},{1,2},{2,3},{4,5},{5,6},{6,7},{8,9},{9,10},{10,11},{12,13},{... | collective-permute-start | bytes 98312 | tf_op jit(solution)/shard_map/cond/branch_2_fun/ppermute | solution.py:493
  33.3 1.3 %collective-permute-start.11 = (bf16[32,512]{1,0:T(8,128)(2,1)S(1)}, bf16[32,512]{1,0:T(8,128)(2,1)S(1)}, u32[]{:S(2)}, u32[]{:S(2)}) collective-permute-start(bf16[32,512]{1,0:T(8,128)(2,1)S(1)} %get-tuple-element.88), channel_id=1, source_target_pairs={{1,0},{2,1},{3,2},{5,4},{6,5},{7,6},{9,8},{10,9},{11,10},{13,12},{... | collective-permute-start | bytes 98312 | tf_op jit(solution)/shard_map/cond/branch_2_fun/ppermute | solution.py:494
  34.6 2.8 %collective-permute-done.10.left_ref = bf16[32,512]{1,0:T(8,128)(2,1)S(1)} collective-permute-done((bf16[32,512]{1,0:T(8,128)(2,1)S(1)}, bf16[32,512]{1,0:T(8,128)(2,1)S(1)}, u32[]{:S(2)}, u32[]{:S(2)}) %collective-permute-start.10) | collective-permute-done | bytes 32800 | tf_op jit(solution)/shard_map/cond/branch_2_fun/ppermute | solution.py:493
  37.4 3.6 %collective-permute-done.11.right_ref = bf16[32,512]{1,0:T(8,128)(2,1)S(1)} collective-permute-done((bf16[32,512]{1,0:T(8,128)(2,1)S(1)}, bf16[32,512]{1,0:T(8,128)(2,1)S(1)}, u32[]{:S(2)}, u32[]{:S(2)}) %collective-permute-start.11) | collective-permute-done | bytes 32800 | tf_op jit(solution)/shard_map/cond/branch_2_fun/ppermute | solution.py:494
  41.1 0.0 copy-done.1
  41.1 0.0 copy-done.4
  41.1 0.0 copy-done.6
  41.1 1.4 %relax.5.base_ref = f32[8,32768]{1,0:T(8,128)S(1)} custom-call(s32[8]{0:T(128)S(1)} %copy-done.4, f32[1,8]{1,0:T(1,128)S(1)} %copy-done.6, f32[8,32768]{1,0:T(8,128)S(1)} %copy-done.1, bf16[32,512]{1,0:T(8,128)(2,1)S(1)} %collective-permute-done.10.left_ref, bf16[32,512]{1,0:T(8,128)(2,1)S(1)} %collective-permute-done.11.right_ref), custom_call_target="tpu_custom_call" | custom-call | flops 10000000 | bytes 4000000 | tf_op jit(solution)/shard_map/cond/branch_2_fun/relax/pallas_call | solution.py:223
  42.4 0.0 collective-permute-done.15.refs_1_
  42.5 0.0 collective-permute-done.16.refs_2_
  42.5 0.0 collective-permute-done.17.refs_3_
  42.5 2.6 %finish.5 = f32[8,32768]{1,0:T(8,128)S(1)} custom-call(s32[8]{0:T(128)S(1)} %copy-done.4, f32[8,32768]{1,0:T(8,128)S(1)} %relax.5.base_ref, bf16[32,8,512]{2,1,0:T(8,128)(2,1)S(1)} %get-tuple-element.89.even_ref, bf16[32,8,512]{2,1,0:T(8,128)(2,1)S(1)} %get-tuple-element.90.odd_ref, bf16[16,8,512]{2,1,0:T(8,128)(2,1)S(1)} %get-tuple-element.93.refs_0_, ...), custom_call_target="tpu_custom_call" | custom-call | flops 1000000 | bytes 3000000 | tf_op jit(solution)/shard_map/cond/branch_2_fun/finish/pallas_call | solution.py:455
  45.1 0.0 copy-start.2
  45.1 1.0 %copy-done.2 = f32[1,8,32768]{2,1,0:T(8,128)} copy-done((f32[1,8,32768]{2,1,0:T(8,128)}, f32[1,8,32768]{2,1,0:T(8,128)S(1)}, u32[]{:S(2)}) %copy-start.2) | copy-done | bytes 1048600
Async XLA Ops:
  2.0 6.4 %collective-permute-start.18 = (bf16[32,8,512]{2,1,0:T(8,128)(2,1)S(1)}, bf16[32,8,512]{2,1,0:T(8,128)(2,1)S(1)}, u32[]{:S(2)}, u32[]{:S(2)}) collective-permute-start(bf16[32,8,512]{2,1,0:T(8,128)(2,1)S(1)} %get-tuple-element.103), channel_id=1, source_target_pairs={{0,4},{4,0},{1,5},{5,1},{2,6},{6,2},{3,7},{7,3},{8,12},{12,8},{9,1... | collective-permute-start | bytes 786440 | tf_op jit(solution)/shard_map/ppermute | solution.py:490
  2.1 8.3 %collective-permute-start.19 = (bf16[32,8,512]{2,1,0:T(8,128)(2,1)S(1)}, bf16[32,8,512]{2,1,0:T(8,128)(2,1)S(1)}, u32[]{:S(2)}, u32[]{:S(2)}) collective-permute-start(bf16[32,8,512]{2,1,0:T(8,128)(2,1)S(1)} %get-tuple-element.104), channel_id=1, source_target_pairs={{4,8},{8,4},{5,9},{9,5},{6,10},{10,6},{7,11},{11,7},{12,16},{16,12... | collective-permute-start | bytes 786440 | tf_op jit(solution)/shard_map/ppermute | solution.py:489
  10.3 30.7 %copy-start.1 = (f32[8,32768]{1,0:T(8,128)S(1)}, f32[8,32768]{1,0:T(8,128)}, u32[]{:S(2)}) copy-start(f32[8,32768]{1,0:T(8,128)} %get-tuple-element.86.cells_ref) | copy-start | bytes 3145732 | tf_op jit(solution)/shard_map/cond
  10.3 30.7 %copy-start.4 = (s32[8]{0:T(128)S(1)}, s32[8]{0:T(128)}, u32[]{:S(2)}) copy-start(s32[8]{0:T(128)} %get-tuple-element.84.level_ref) | copy-start | bytes 100 | tf_op jit(solution)/shard_map/cond
  10.3 30.7 %copy-start.6 = (f32[1,8]{1,0:T(1,128)S(1)}, f32[1,8]{1,0:T(1,128)}, u32[]{:S(2)}) copy-start(f32[1,8]{1,0:T(1,128)} %get-tuple-element.85.rate_ref) | copy-start | bytes 100 | tf_op jit(solution)/shard_map/cond
  11.2 5.7 %collective-permute-start.14 = (bf16[8,8,512]{2,1,0:T(8,128)(2,1)S(1)}, bf16[8,8,512]{2,1,0:T(8,128)(2,1)S(1)}, u32[]{:S(2)}, u32[]{:S(2)}) collective-permute-start(bf16[8,8,512]{2,1,0:T(8,128)(2,1)S(1)} %coarse_piece.1.refs_0_), channel_id=1, source_target_pairs={{0,3},{1,0},{2,1},{3,2},{4,7},{5,4},{6,5},{7,6},{8,11},{9,8},{10,9... | collective-permute-start | bytes 196616 | tf_op jit(solution)/shard_map/cond/branch_2_fun/ppermute | solution.py:480
  15.0 7.8 %collective-permute-start.13 = (bf16[8,8,512]{2,1,0:T(8,128)(2,1)S(1)}, bf16[8,8,512]{2,1,0:T(8,128)(2,1)S(1)}, u32[]{:S(2)}, u32[]{:S(2)}) collective-permute-start(bf16[8,8,512]{2,1,0:T(8,128)(2,1)S(1)} %coarse_piece.1.refs_0_), channel_id=1, source_target_pairs={{0,2},{1,3},{2,0},{3,1},{4,6},{5,7},{6,4},{7,5},{8,10},{9,11},{10,... | collective-permute-start | bytes 196616 | tf_op jit(solution)/shard_map/cond/branch_2_fun/ppermute | solution.py:480
  15.0 7.8 %collective-permute-start.12 = (bf16[8,8,512]{2,1,0:T(8,128)(2,1)S(1)}, bf16[8,8,512]{2,1,0:T(8,128)(2,1)S(1)}, u32[]{:S(2)}, u32[]{:S(2)}) collective-permute-start(bf16[8,8,512]{2,1,0:T(8,128)(2,1)S(1)} %coarse_piece.1.refs_0_), channel_id=1, source_target_pairs={{0,1},{1,2},{2,3},{3,0},{4,5},{5,6},{6,7},{7,4},{8,9},{9,10},{10,1... | collective-permute-start | bytes 196616 | tf_op jit(solution)/shard_map/cond/branch_2_fun/ppermute | solution.py:480
  23.6 18.8 %collective-permute-start.15 = (bf16[16,8,512]{2,1,0:T(8,128)(2,1)S(1)}, bf16[16,8,512]{2,1,0:T(8,128)(2,1)S(1)}, u32[]{:S(2)}, u32[]{:S(2)}) collective-permute-start(bf16[16,8,512]{2,1,0:T(8,128)(2,1)S(1)} %get-tuple-element.94), channel_id=1, source_target_pairs={{0,3},{1,0},{2,1},{3,2},{4,7},{5,4},{6,5},{7,6},{8,11},{9,8},{10,9... | collective-permute-start | bytes 393224 | tf_op jit(solution)/shard_map/cond/branch_2_fun/ppermute | solution.py:480
  27.3 15.2 %collective-permute-start.16 = (bf16[16,8,512]{2,1,0:T(8,128)(2,1)S(1)}, bf16[16,8,512]{2,1,0:T(8,128)(2,1)S(1)}, u32[]{:S(2)}, u32[]{:S(2)}) collective-permute-start(bf16[16,8,512]{2,1,0:T(8,128)(2,1)S(1)} %get-tuple-element.95), channel_id=1, source_target_pairs={{0,2},{1,3},{2,0},{3,1},{4,6},{5,7},{6,4},{7,5},{8,10},{9,11},{10,... | collective-permute-start | bytes 393224 | tf_op jit(solution)/shard_map/cond/branch_2_fun/ppermute | solution.py:480
  29.5 13.0 %collective-permute-start.17 = (bf16[16,8,512]{2,1,0:T(8,128)(2,1)S(1)}, bf16[16,8,512]{2,1,0:T(8,128)(2,1)S(1)}, u32[]{:S(2)}, u32[]{:S(2)}) collective-permute-start(bf16[16,8,512]{2,1,0:T(8,128)(2,1)S(1)} %get-tuple-element.96), channel_id=1, source_target_pairs={{0,1},{1,2},{2,3},{3,0},{4,5},{5,6},{6,7},{7,4},{8,9},{9,10},{10,1... | collective-permute-start | bytes 393224 | tf_op jit(solution)/shard_map/cond/branch_2_fun/ppermute | solution.py:480
  31.4 6.0 %collective-permute-start.10 = (bf16[32,512]{1,0:T(8,128)(2,1)S(1)}, bf16[32,512]{1,0:T(8,128)(2,1)S(1)}, u32[]{:S(2)}, u32[]{:S(2)}) collective-permute-start(bf16[32,512]{1,0:T(8,128)(2,1)S(1)} %get-tuple-element.87), channel_id=1, source_target_pairs={{0,1},{1,2},{2,3},{4,5},{5,6},{6,7},{8,9},{9,10},{10,11},{12,13},{... | collective-permute-start | bytes 98312 | tf_op jit(solution)/shard_map/cond/branch_2_fun/ppermute | solution.py:493
  33.3 7.7 %collective-permute-start.11 = (bf16[32,512]{1,0:T(8,128)(2,1)S(1)}, bf16[32,512]{1,0:T(8,128)(2,1)S(1)}, u32[]{:S(2)}, u32[]{:S(2)}) collective-permute-start(bf16[32,512]{1,0:T(8,128)(2,1)S(1)} %get-tuple-element.88), channel_id=1, source_target_pairs={{1,0},{2,1},{3,2},{5,4},{6,5},{7,6},{9,8},{10,9},{11,10},{13,12},{... | collective-permute-start | bytes 98312 | tf_op jit(solution)/shard_map/cond/branch_2_fun/ppermute | solution.py:494
  45.1 1.0 %copy-start.2 = (f32[1,8,32768]{2,1,0:T(8,128)}, f32[1,8,32768]{2,1,0:T(8,128)S(1)}, u32[]{:S(2)}) copy-start(f32[1,8,32768]{2,1,0:T(8,128)S(1)} %get-tuple-element.146) | copy-start | bytes 3145732
